TPU v7x, 32 devices: a whole 2x2x4 slice. The times are simulated.
32 devices in a mesh: dp: 4 (over x, core), group: 4 (over z), tensor: 2 (over y).
Axes of the slice: x: 2, y: 2, z: 4, core: 2. Of those that a mesh axis runs over, the one named last changes fastest.
Arguments:
- residual_in: bfloat16 [32, 1024, 767], P(('dp', 'group'), 'tensor'), may hold values from -6 to 6
- piece_ids: int32 [32, 1024], P(('dp', 'group')), may hold values from -1 to 3, as said below
- norm_gains: bfloat16 [2, 768], replicated, may hold values from 0.25 to 1.75
- qkv_weight: bfloat16 [3, 768, 768], P(None, None, 'tensor'), may hold values from -0.21875 to 0.21875
- qv_bias: bfloat16 [2, 768], P(None, 'tensor'), may hold values from -3 to 3
- out_weight: bfloat16 [768, 767], P('tensor'), may hold values from -0.875 to 0.875
- fc_weight: bfloat16 [768, 3072], P(None, 'tensor'), may hold values from -0.21875 to 0.21875
- fc_bias: bfloat16 [3072], P('tensor'), may hold values from -3 to 3
- proj_weight: bfloat16 [3072, 767], P('tensor'), may hold values from -0.109375 to 0.109375
- out_biases: bfloat16 [2, 767], replicated, may hold values from -2 to 2
- cotangent: bfloat16 [32, 1024, 767], P(('dp', 'group'), 'tensor'), may hold values from -6 to 6
Outputs:
- block_out: bfloat16 [32, 1024, 767], P(('dp', 'group'), 'tensor')
- grad_input: bfloat16 [32, 1024, 767], P(('dp', 'group'), 'tensor')
- grad_gains: float32 [2, 768], replicated
- grad_qkv: float32 [3, 768, 768], P(None, 'dp', 'tensor')
- grad_qv_bias: float32 [2, 768], P(None, ('tensor', 'dp'))
- grad_out_weight: float32 [768, 767], P(('tensor', 'dp'))
- grad_fc_weight: float32 [768, 3072], P('dp', 'tensor')
- grad_fc_bias: float32 [3072], P(('tensor', 'dp'))
- grad_proj_weight: float32 [3072, 767], P(('tensor', 'dp'))
- grad_out_biases: float32 [2, 767], replicated
Inputs may be any that keep to these rules, and one draw needn't show every extreme that they name: `piece_ids`: each aligned block of 256 positions of a sequence carries one id: -1 (text) or the block's own number (a picture piece). The first block of every sequence is text and the last one a picture piece.
All inputs are finite; a program needn't handle non-finite values.
Results may differ from a plain program's by a relative error of at most 0.02.
Values may be sent and summed in bfloat16 or wider, within the bound.
No kernel may reach another device: no remote copies, remote signals or barrier semaphores. Data moves between devices by JAX's collectives and lax.ppermute only.
A program may use at most 192 MiB of HBM per device.

v0:
```python
import jax
import jax.numpy as jnp
from jax import lax
from jax.sharding import PartitionSpec as P

D = 768
HD = 64
EPSILON = 1e-05
MASKED = -1e30


def decompress(compact):
    return jnp.concatenate([compact, -jnp.sum(compact, axis=-1, keepdims=True)], axis=-1)


def crms_gain(compact, gain):
    full_rows = decompress(compact)
    factor = lax.rsqrt(jnp.mean(full_rows * full_rows, axis=-1, keepdims=True) + EPSILON)
    return full_rows * factor * gain


def gelu_tanh(values):
    return jax.nn.gelu(values, approximate=True)


def visible_mask(labels, row_start, row_count):
    query_pos = row_start + jnp.arange(row_count)
    key_pos = jnp.arange(labels.shape[0])
    row_labels = labels[row_start : row_start + row_count]
    causal = key_pos[None, :] <= query_pos[:, None]
    inside = (row_labels[:, None] == labels[None, :]) & (row_labels[:, None] >= 0)
    return causal | inside


def block_scores(row_query, key_rows, labels, row_start, row_block):
    scores = jnp.einsum(
        "qhd,khd->hqk", row_query, key_rows, preferred_element_type=jnp.float32
    ) * HD ** (-0.5)
    return jnp.where(visible_mask(labels, row_start, row_block)[None], scores, MASKED)


def attend_forward(inputs):
    queries, key_rows, value_rows, labels = inputs
    length = key_rows.shape[0]
    row_block = min(512, length)
    outputs = []
    log_parts = []
    for row_start in range(0, length, row_block):
        scores = block_scores(
            queries[row_start : row_start + row_block], key_rows, labels, row_start, row_block
        )
        highest = jnp.max(scores, axis=-1, keepdims=True)
        weights = jnp.exp(scores - highest)
        weight_sum = jnp.sum(weights, axis=-1, keepdims=True)
        prob_low = (weights / weight_sum).astype(jnp.bfloat16)
        outputs.append(
            jnp.einsum(
                "hqk,khd->qhd", prob_low, value_rows, preferred_element_type=jnp.float32
            ).astype(jnp.bfloat16)
        )
        log_parts.append((highest + jnp.log(weight_sum))[..., 0])
    return (jnp.concatenate(outputs, 0), jnp.concatenate(log_parts, 1))


def attend_backward(inputs):
    queries, key_rows, value_rows, labels, upstream, log_sums = inputs
    length = key_rows.shape[0]
    row_block = min(512, length)
    score_scale = HD ** (-0.5)
    grad_keys = jnp.zeros(key_rows.shape, jnp.float32)
    grad_values = jnp.zeros(value_rows.shape, jnp.float32)
    query_grads = []
    for row_start in range(0, length, row_block):
        row_query = queries[row_start : row_start + row_block]
        row_up = upstream[row_start : row_start + row_block]
        scores = block_scores(row_query, key_rows, labels, row_start, row_block)
        probs = jnp.exp(scores - log_sums[:, row_start : row_start + row_block, None])
        along = jnp.einsum("qhd,khd->hqk", row_up, value_rows, preferred_element_type=jnp.float32)
        inner = jnp.sum(along * probs, axis=-1, keepdims=True)
        score_grad = (probs * (along - inner)).astype(jnp.bfloat16)
        query_grads.append(
            jnp.einsum("hqk,khd->qhd", score_grad, key_rows, preferred_element_type=jnp.float32)
            * score_scale
        )
        grad_keys = (
            grad_keys
            + jnp.einsum("hqk,qhd->khd", score_grad, row_query, preferred_element_type=jnp.float32)
            * score_scale
        )
        grad_values = grad_values + jnp.einsum(
            "hqk,qhd->khd", probs.astype(jnp.bfloat16), row_up, preferred_element_type=jnp.float32
        )
    return (jnp.concatenate(query_grads, 0), grad_keys, grad_values)


def on_device(
    residual_in,
    piece_ids,
    norm_gains,
    qkv_weight,
    qv_bias,
    out_weight,
    fc_weight,
    fc_bias,
    proj_weight,
    out_biases,
    cotangent,
):
    residual_rows, upstream_rows, labels_all = (residual_in, cotangent, piece_ids)
    qkv_w, qv_b, out_w, fc_w, fc_b, proj_w = (
        qkv_weight,
        qv_bias,
        out_weight,
        fc_weight,
        fc_bias,
        proj_weight,
    )
    seq_count, local_len, compact_width = residual_rows.shape
    local_rows = seq_count * local_len
    local_width = qkv_w.shape[2]
    head_count = local_width // HD
    gain_values = norm_gains.astype(jnp.float32)
    bias_values = qv_b.astype(jnp.float32)
    end_biases = out_biases.astype(jnp.float32)
    inputs_flat = residual_rows.reshape(local_rows, compact_width).astype(jnp.float32)
    normed_one, norm_one_back = jax.vjp(crms_gain, inputs_flat, gain_values[0])
    one_low = normed_one.astype(jnp.bfloat16).reshape(seq_count, local_len, D)
    full_one = lax.all_gather(one_low, "tensor", axis=1, tiled=True)
    seq_len = full_one.shape[1]
    token_count = seq_count * seq_len
    flat_one = full_one.reshape(token_count, D)
    projected = jnp.einsum("td,cde->cte", flat_one, qkv_w, preferred_element_type=jnp.float32)
    queries = (
        (projected[0] + bias_values[0])
        .astype(jnp.bfloat16)
        .reshape(seq_count, seq_len, head_count, HD)
    )
    key_rows = projected[1].astype(jnp.bfloat16).reshape(seq_count, seq_len, head_count, HD)
    value_rows = (
        (projected[2] + bias_values[1])
        .astype(jnp.bfloat16)
        .reshape(seq_count, seq_len, head_count, HD)
    )
    attended, log_sums = lax.map(attend_forward, (queries, key_rows, value_rows, labels_all))
    attended_flat = attended.reshape(token_count, local_width)
    branch_part = jnp.dot(attended_flat, out_w, preferred_element_type=jnp.float32).reshape(
        seq_count, seq_len, compact_width
    )
    branch_sum = lax.psum_scatter(
        branch_part.astype(jnp.bfloat16), "tensor", scatter_dimension=1, tiled=True
    ).astype(jnp.float32)
    middle = inputs_flat + branch_sum.reshape(local_rows, compact_width) + end_biases[0]
    normed_two, norm_two_back = jax.vjp(crms_gain, middle, gain_values[1])
    two_low = normed_two.astype(jnp.bfloat16).reshape(seq_count, local_len, D)
    full_two = lax.all_gather(two_low, "tensor", axis=1, tiled=True).reshape(token_count, D)
    hidden_pre = jnp.dot(full_two, fc_w, preferred_element_type=jnp.float32) + fc_b.astype(
        jnp.float32
    )
    active_full, gelu_back = jax.vjp(gelu_tanh, hidden_pre)
    active = active_full.astype(jnp.bfloat16)
    mlp_part = jnp.dot(active, proj_w, preferred_element_type=jnp.float32).reshape(
        seq_count, seq_len, compact_width
    )
    mlp_sum = lax.psum_scatter(
        mlp_part.astype(jnp.bfloat16), "tensor", scatter_dimension=1, tiled=True
    ).astype(jnp.float32)
    block_out = (
        (middle + mlp_sum.reshape(local_rows, compact_width) + end_biases[1])
        .astype(jnp.bfloat16)
        .reshape(seq_count, local_len, compact_width)
    )
    upstream_full = lax.all_gather(upstream_rows, "tensor", axis=1, tiled=True).reshape(
        token_count, compact_width
    )
    upstream_flat = upstream_rows.reshape(local_rows, compact_width).astype(jnp.float32)
    grad_proj_weight = jnp.dot(active.T, upstream_full, preferred_element_type=jnp.float32)
    hidden_grad = gelu_back(jnp.dot(upstream_full, proj_w.T, preferred_element_type=jnp.float32))[
        0
    ].astype(jnp.bfloat16)
    grad_fc_weight = jnp.dot(full_two.T, hidden_grad, preferred_element_type=jnp.float32)
    grad_fc_bias = jnp.sum(hidden_grad.astype(jnp.float32), axis=0)
    two_part = jnp.dot(hidden_grad, fc_w.T, preferred_element_type=jnp.float32).reshape(
        seq_count, seq_len, D
    )
    two_grad = (
        lax.psum_scatter(two_part.astype(jnp.bfloat16), "tensor", scatter_dimension=1, tiled=True)
        .astype(jnp.float32)
        .reshape(local_rows, D)
    )
    middle_norm_grad, gain_two_grad = norm_two_back(two_grad)
    middle_grad = upstream_flat + middle_norm_grad
    branch_low = middle_grad.astype(jnp.bfloat16)
    branch_seq = branch_low.reshape(seq_count, local_len, compact_width)
    branch_full = lax.all_gather(branch_seq, "tensor", axis=1, tiled=True).reshape(
        token_count, compact_width
    )
    grad_out_weight = jnp.dot(attended_flat.T, branch_full, preferred_element_type=jnp.float32)
    attended_grad = (
        jnp.dot(branch_full, out_w.T, preferred_element_type=jnp.float32)
        .astype(jnp.bfloat16)
        .reshape(seq_count, seq_len, head_count, HD)
    )
    query_grad, key_grad, value_grad = lax.map(
        attend_backward, (queries, key_rows, value_rows, labels_all, attended_grad, log_sums)
    )
    stacked = (
        jnp.stack([query_grad, key_grad, value_grad])
        .astype(jnp.bfloat16)
        .reshape(3, token_count, local_width)
    )
    grad_qkv = jnp.einsum("td,cte->cde", flat_one, stacked, preferred_element_type=jnp.float32)
    grad_qv_bias = jnp.stack(
        [
            jnp.sum(stacked[0].astype(jnp.float32), axis=0),
            jnp.sum(stacked[2].astype(jnp.float32), axis=0),
        ]
    )
    one_part = jnp.einsum(
        "cte,cde->td", stacked, qkv_w, preferred_element_type=jnp.float32
    ).reshape(seq_count, seq_len, D)
    one_grad = (
        lax.psum_scatter(one_part.astype(jnp.bfloat16), "tensor", scatter_dimension=1, tiled=True)
        .astype(jnp.float32)
        .reshape(local_rows, D)
    )
    input_norm_grad, gain_one_grad = norm_one_back(one_grad)
    grad_input = (
        (middle_grad + input_norm_grad)
        .astype(jnp.bfloat16)
        .reshape(seq_count, local_len, compact_width)
    )
    gain_terms = jnp.stack([gain_one_grad, gain_two_grad])
    bias_terms = jnp.stack(
        [jnp.sum(branch_low.astype(jnp.float32), axis=0), jnp.sum(upstream_flat, axis=0)]
    )
    grad_gains, grad_out_biases = lax.psum((gain_terms, bias_terms), ("dp", "group", "tensor"))
    weight_grads = (
        grad_qkv,
        grad_qv_bias,
        grad_out_weight,
        grad_fc_weight,
        grad_fc_bias,
        grad_proj_weight,
    )
    shards = (
        lax.psum_scatter(
            weight_grads[0].astype(jnp.bfloat16), "dp", scatter_dimension=1, tiled=True
        ).astype(jnp.float32),
        lax.psum_scatter(
            weight_grads[1].astype(jnp.bfloat16), "dp", scatter_dimension=1, tiled=True
        ).astype(jnp.float32),
        lax.psum_scatter(
            weight_grads[2].astype(jnp.bfloat16), "dp", scatter_dimension=0, tiled=True
        ).astype(jnp.float32),
        lax.psum_scatter(
            weight_grads[3].astype(jnp.bfloat16), "dp", scatter_dimension=0, tiled=True
        ).astype(jnp.float32),
        lax.psum_scatter(
            weight_grads[4].astype(jnp.bfloat16), "dp", scatter_dimension=0, tiled=True
        ).astype(jnp.float32),
        lax.psum_scatter(
            weight_grads[5].astype(jnp.bfloat16), "dp", scatter_dimension=0, tiled=True
        ).astype(jnp.float32),
    )
    reduced = (
        lax.psum(shards[0].astype(jnp.bfloat16), "group").astype(jnp.float32),
        lax.psum(shards[1].astype(jnp.bfloat16), "group").astype(jnp.float32),
        lax.psum(shards[2].astype(jnp.bfloat16), "group").astype(jnp.float32),
        lax.psum(shards[3].astype(jnp.bfloat16), "group").astype(jnp.float32),
        lax.psum(shards[4].astype(jnp.bfloat16), "group").astype(jnp.float32),
        lax.psum(shards[5].astype(jnp.bfloat16), "group").astype(jnp.float32),
    )
    return (
        block_out,
        grad_input,
        grad_gains,
        reduced[0],
        reduced[1],
        reduced[2],
        reduced[3],
        reduced[4],
        reduced[5],
        grad_out_biases,
    )


def solution(mesh):
    in_specs = (
        P(("dp", "group"), "tensor", None),
        P(("dp", "group"), None),
        P(),
        P(None, None, "tensor"),
        P(None, "tensor"),
        P("tensor", None),
        P(None, "tensor"),
        P("tensor"),
        P("tensor", None),
        P(),
        P(("dp", "group"), "tensor", None),
    )
    out_specs = (
        P(("dp", "group"), "tensor", None),
        P(("dp", "group"), "tensor", None),
        P(),
        P(None, "dp", "tensor"),
        P(None, ("tensor", "dp")),
        P(("tensor", "dp"), None),
        P("dp", "tensor"),
        P(("tensor", "dp")),
        P(("tensor", "dp"), None),
        P(),
    )
    return jax.shard_map(
        on_device, mesh=mesh, in_specs=in_specs, out_specs=out_specs, check_vma=False
    )
```

profile of v0, /device:TPU:0, one launch (start us, length us, event | category | flops | bytes accessed | tf_op | source)
XLA Modules:
  0.0 1026.2 jit_solution(11230917446306738538)
XLA Ops:
  28.7 47.5 %all-gather.5.cloned.1.call-done = bf16[2,1024,768]{2,1,0:T(8,128)(2,1)} async-done(((bf16[2,512,768]{2,1,0:T(8,128)(2,1)}), bf16[2,1024,768]{2,1,0:T(8,128)(2,1)}) %all-gather.5.cloned.1.call-update) | async-done | bytes 3145744 | tf_op jit(solution)/shard_map/all_gather | solution.py:128
  124.6 54.4 %while.26 = (s32[]{:T(128)}, bf16[2,1024,6,64]{1,3,2,0:T(8,128)(2,1)}, f32[2,6,1024]{2,1,0:T(8,128)}, bf16[2,1024,6,64]{1,3,2,0:T(8,128)(2,1)}, s32[2,1024]{1,0:...) while((s32[]{:T(128)}, ...), condition=%wide.region_7.8_spmd, body=%wide.region_2.7_spmd.sunk | while | flops 1692272128 | bytes 111457016 | solution.py:144
  185.3 42.1 %reduce-scatter.14.cloned.1.call-done = bf16[2,512,767]{2,1,0:T(8,128)(2,1)} async-done(((bf16[2,1024,767]{2,1,0:T(8,128)(2,1)}), bf16[2,512,767]{2,1,0:T(8,128)(2,1)}) %reduce-scatter.14.cloned.1.call-update) | async-done | bytes 1570832 | tf_op jit(solution)/shard_map/reduce_scatter | solution.py:149
  244.4 29.4 %all-gather.9.cloned.1.call-done = bf16[2,1024,767]{1,0,2:T(2,128)(2,1)} async-done(((bf16[2,512,767]{1,0,2:T(2,128)(2,1)}), bf16[2,1024,767]{1,0,2:T(2,128)(2,1)}) %all-gather.9.cloned.1.call-update) | async-done | bytes 3141648 | tf_op jit(solution)/shard_map/all_gather | solution.py:172
  280.9 39.4 %all-gather.7.cloned.1.call-done = bf16[2,1024,768]{2,1,0:T(8,128)(2,1)} async-done(((bf16[2,512,768]{2,1,0:T(8,128)(2,1)}), bf16[2,1024,768]{2,1,0:T(8,128)(2,1)}) %all-gather.7.cloned.1.call-update) | async-done | bytes 3145744 | tf_op jit(solution)/shard_map/all_gather | solution.py:155
  320.3 13.8 %multiply_convert_fusion.2 = (bf16[2048,1536]{1,0:T(8,128)(2,1)}, f32[2048,1536]{1,0:T(8,128)}) fusion(f32[1536]{0:T(1024)S(1)} %convert_element_type.208, bf16[2048,768]{1,0:T(8,128)(2,1)} %bitcast.353, bf16[768,1536]{1,0:T(8,128)(2,1)S(1)} %copy-done), kind=kOutput, calls=%fused_computation.125 | convolution fusion | flops 4863295488 | bytes 24385536 | tf_op jit(solution)/shard_map/dot_general | solution.py:156
  334.1 15.3 %fusion.97 = (bf16[1536]{0:T(1024)(128)(2,1)}, bf16[2048,1536]{1,0:T(8,128)(2,1)S(1)}) fusion(f32[2048,1536]{1,0:T(8,128)} %get-tuple-element.273, f32[1536]{0:T(1024)S(1)} %convert_element_type.208, bf16[2048,767]{0,1:T(8,128)(2,1)S(1)} %bitcast.318, bf16[1536,767]{1,0:T(8,128)(2,1)S(1)} %copy-done.63), kind=kOutput, calls=%fused_computation.195 | convolution fusion | flops 4894751232 | bytes 24381440 | tf_op jit(solution)/shard_map/dot_general | solution.py:177
  362.0 37.4 %reduce-scatter.18.cloned.1.call-done = bf16[2,512,768]{2,1,0:T(8,128)(2,1)} async-done(((bf16[2,1024,768]{2,1,0:T(8,128)(2,1)}), bf16[2,512,768]{2,1,0:T(8,128)(2,1)}) %reduce-scatter.18.cloned.1.call-update) | async-done | bytes 1572880 | tf_op jit(solution)/shard_map/reduce_scatter | solution.py:186
  412.4 44.9 %all-gather.11.cloned.1.call-done = bf16[2,1024,767]{1,0,2:T(2,128)(2,1)} async-done(((bf16[2,512,767]{1,0,2:T(2,128)(2,1)}), bf16[2,1024,767]{1,0,2:T(2,128)(2,1)}) %all-gather.11.cloned.1.call-update) | async-done | bytes 3141648 | tf_op jit(solution)/shard_map/all_gather | solution.py:194
  472.5 133.8 %while.27 = (s32[]{:T(128)}, bf16[2,1024,6,64]{1,3,2,0:T(8,128)(2,1)}, bf16[2,1024,6,64]{1,3,2,0:T(8,128)(2,1)}, bf16[2,1024,6,64]{1,3,2,0:T(8,128)(2,1)}, bf16[...) while((s32[]{:T(128)}, ...), condition=%wide.region_17.18_spmd, body=%wide.region_14.17_spmd.sunk | while | flops 4128632320 | bytes 286275584 | solution.py:203
  492.8 8.4 multiply_reduce_fusion.10
  501.2 9.6 multiply_convert_fusion.7
  516.0 8.1 multiply_reduce_fusion.11
  524.1 7.0 multiply_convert_fusion.8
  559.4 8.4 multiply_reduce_fusion.10
  567.8 9.6 multiply_convert_fusion.7
  582.7 8.1 multiply_reduce_fusion.11
  590.8 7.0 multiply_convert_fusion.8
  638.5 9.4 convolution_convert_fusion
  648.0 9.4 convolution_convert_fusion.1
  663.5 9.0 convolution_convert_fusion.3
  678.5 25.3 %reduce-scatter.26.cloned.1.call-done = bf16[384,767]{1,0:T(8,128)(2,1)} async-done(((bf16[1536,767]{1,0:T(8,128)(2,1)}), bf16[384,767]{1,0:T(8,128)(2,1)}) %reduce-scatter.26.cloned.1.call-update) | async-done | bytes 589072 | tf_op jit(solution)/shard_map/reduce_scatter | solution.py:261
  703.8 35.6 %reduce-scatter.24.cloned.1.call-done = bf16[192,1536]{1,0:T(8,128)(2,1)} async-done(((bf16[768,1536]{1,0:T(8,128)(2,1)}), bf16[192,1536]{1,0:T(8,128)(2,1)}) %reduce-scatter.24.cloned.1.call-update) | async-done | bytes 589840 | tf_op jit(solution)/shard_map/reduce_scatter | solution.py:255
  739.4 25.2 %reduce-scatter.22.cloned.1.call-done = bf16[96,767]{1,0:T(8,128)(2,1)} async-done(((bf16[384,767]{1,0:T(8,128)(2,1)}), bf16[96,767]{1,0:T(8,128)(2,1)}) %reduce-scatter.22.cloned.1.call-update) | async-done | bytes 147280 | tf_op jit(solution)/shard_map/reduce_scatter | solution.py:252
  764.7 7.0 copy.87
  771.7 9.1 bitcast_convert_fusion
  792.0 18.4 %reduce-scatter.16.cloned.1.call-done = bf16[2,512,767]{2,1,0:T(8,128)(2,1)} async-done(((bf16[2,1024,767]{2,1,0:T(8,128)(2,1)}), bf16[2,512,767]{2,1,0:T(8,128)(2,1)}) %reduce-scatter.16.cloned.1.call-update) | async-done | bytes 1570832 | tf_op jit(solution)/shard_map/reduce_scatter | solution.py:164
  818.3 14.5 %reduce-scatter.30.cloned.1.call-done = bf16[96,2]{1,0:T(8,128)(2,1)} async-done(((bf16[384,2]{1,0:T(8,128)(2,1)}), bf16[96,2]{1,0:T(8,128)(2,1)}) %reduce-scatter.30.cloned.1.call-update) | async-done | bytes 400
  833.6 11.8 %all-reduce.2 = (bf16[2,96]{1,0:T(2,128)(2,1)S(1)}, bf16[384]{0:T(512)(128)(2,1)S(1)}) all-reduce(bf16[2,96]{1,0:T(2,128)(2,1)S(1)} %copy.97, bf16[384]{0:T(512)(128)(2,1)S(1)} %dynamic-slice.1), channel_id=1, replica_groups=mesh['dp'=4,'group'=4,'tensor'=2] {'group'}, use_global_device_ids=true, to_apply=%region_28.29 | all-reduce | flops 576 | bytes 2304 | tf_op jit(solution)/shard_map/psum | solution.py:267
  846.5 71.2 %all-reduce.6.cloned.1.call-done = (bf16[3,192,384]{1,2,0:T(8,128)(2,1)}, bf16[96,767]{1,0:T(8,128)(2,1)}, bf16[192,1536]{1,0:T(8,128)(2,1)}, bf16[384,767]{1,0:T(8,128)(2,1)}) async-done(((bf16[3,192,384]{1,2,0:T(8,128)(2,1)}, bf16[96,767]{1,0:T(8,128)(2,1)}, bf16[192,1536]{1,0:T(8,128)(2,1)}, bf16[384,767]{1,0:T(8,128)(2,1)}), (bf16[3,192,384]{1,2,0:T(8,128)(2,1)}, bf16[96,767]{1,0:T(8,128)(2,1)}, ...) | async-done | bytes 1768528 | tf_op jit(solution)/shard_map/psum | solution.py:266
  926.1 36.2 %reduce-scatter.20.cloned.1.call-done = bf16[2,512,768]{2,1,0:T(8,128)(2,1)} async-done(((bf16[2,1024,768]{2,1,0:T(8,128)(2,1)}), bf16[2,512,768]{2,1,0:T(8,128)(2,1)}) %reduce-scatter.20.cloned.1.call-update) | async-done | bytes 1572880 | tf_op jit(solution)/shard_map/reduce_scatter | solution.py:222
  979.7 39.6 %all-reduce.1 = (f32[2,768]{1,0:T(2,128)}, f32[2,767]{1,0:T(2,128)}) all-reduce(f32[2,768]{1,0:T(2,128)S(1)} %pad_maximum_fusion.4, f32[2,767]{1,0:T(2,128)S(1)} %pad_maximum_fusion.5), channel_id=1, replica_groups=mesh['dp'=4,'group'=4,'tensor'=2] {'dp','group','tensor'}, use_global_device_ids=true, to_apply=%region_22.23 | all-reduce | flops 3070 | bytes 24560 | tf_op jit(solution)/shard_map/psum | solution.py:236
  (387 shorter events, 351.3 us)
Async XLA Ops:
  7.2 313.1 %copy-start = (bf16[768,1536]{1,0:T(8,128)(2,1)S(1)}, bf16[768,1536]{1,0:T(8,128)(2,1)}, u32[]{:S(2)}) copy-start(bf16[768,1536]{1,0:T(8,128)(2,1)} %param.21) | copy-start | bytes 7077892
  7.2 69.0 %all-gather.5.cloned.1.call-start = ((), (), s32[]{:S(2)}) async-start(), calls=%async_computation.9 | async-start | bytes 4718592 | tf_op jit(solution)/shard_map/all_gather | solution.py:128
  28.4 199.0 %reduce-scatter.14.cloned.1.call-start = ((), (), s32[]{:S(2)}) async-start(), calls=%async_computation.10 | async-start | bytes 4718592 | tf_op jit(solution)/shard_map/reduce_scatter | solution.py:149
  124.6 54.4 %copy-start.65 = (bf16[384,767]{1,0:T(8,128)(2,1)S(1)}, bf16[384,767]{1,0:T(8,128)(2,1)}, u32[]{:S(2)}) copy-start(bf16[384,767]{1,0:T(8,128)(2,1)} %param.20) | copy-start | bytes 1767172
  183.9 90.0 %all-gather.9.cloned.1.call-start = ((), (), s32[]{:S(2)}) async-start(), calls=%async_computation.13 | async-start | bytes 4712448 | tf_op jit(solution)/shard_map/all_gather | solution.py:172
  184.6 135.7 %all-gather.7.cloned.1.call-start = ((), (), s32[]{:S(2)}) async-start(), calls=%async_computation.11 | async-start | bytes 4718592 | tf_op jit(solution)/shard_map/all_gather | solution.py:155
  231.6 9.2 copy-start.32
  244.4 155.0 %reduce-scatter.18.cloned.1.call-start = ((), (), s32[]{:S(2)}) async-start(), calls=%async_computation.14 | async-start | bytes 4718592 | tf_op jit(solution)/shard_map/reduce_scatter | solution.py:186
  320.3 13.8 %copy-start.33 = (bf16[96,8,2,1024]{3,1,2,0:T(8,128)(2,1)S(1)}, bf16[96,8,2,1024]{3,1,2,0:T(8,128)(2,1)}, u32[]{:S(2)}) copy-start(bf16[96,8,2,1024]{3,1,2,0:T(8,128)(2,1)} %copy.101) | copy-start | bytes 9437188
  320.3 13.8 %copy-start.63 = (bf16[1536,767]{1,0:T(8,128)(2,1)S(1)}, bf16[1536,767]{1,0:T(8,128)(2,1)}, u32[]{:S(2)}) copy-start(bf16[1536,767]{1,0:T(8,128)(2,1)} %param.23) | copy-start | bytes 7068676
  355.9 101.4 %all-gather.11.cloned.1.call-start = ((), (), s32[]{:S(2)}) async-start(), calls=%async_computation.15 | async-start | bytes 4712448 | tf_op jit(solution)/shard_map/all_gather | solution.py:194
  359.5 39.9 %copy-start.11 = (f32[2,512,767]{2,1,0:T(8,128)S(1)}, f32[2,512,767]{2,1,0:T(8,128)}, u32[]{:S(2)}) copy-start(f32[2,512,767]{2,1,0:T(8,128)} %get-tuple-element.243) | copy-start | bytes 9424900
  412.3 263.4 %reduce-scatter.28.cloned.1.call-start = ((), (), s32[]{:S(2)}) async-start(), calls=%async_computation.20 | async-start | bytes 2211840
  476.6 10.7 %copy-start.5 = (pred[512,1024]{1,0:T(8,128)(4,1)}, pred[512,1024]{1,0:T(8,128)(4,1)S(1)}, u32[]{:S(2)}) copy-start(pred[512,1024]{1,0:T(8,128)(4,1)S(1)} %get-tuple-element.421) | copy-start | bytes 1572868 | tf_op jit(solution)/shard_map/while
  524.1 7.0 copy-start.4
  543.2 10.7 %copy-start.5 = (pred[512,1024]{1,0:T(8,128)(4,1)}, pred[512,1024]{1,0:T(8,128)(4,1)S(1)}, u32[]{:S(2)}) copy-start(pred[512,1024]{1,0:T(8,128)(4,1)S(1)} %get-tuple-element.421) | copy-start | bytes 1572868 | tf_op jit(solution)/shard_map/while
  638.5 65.3 %reduce-scatter.26.cloned.1.call-start = ((), (), s32[]{:S(2)}) async-start(), calls=%async_computation.19 | async-start | bytes 2949120 | tf_op jit(solution)/shard_map/reduce_scatter | solution.py:261
  638.5 9.4 copy-start.62
  647.9 91.5 %reduce-scatter.24.cloned.1.call-start = ((), (), s32[]{:S(2)}) async-start(), calls=%async_computation.18 | async-start | bytes 2949120 | tf_op jit(solution)/shard_map/reduce_scatter | solution.py:255
  657.4 107.2 %reduce-scatter.22.cloned.1.call-start = ((), (), s32[]{:S(2)}) async-start(), calls=%async_computation.17 | async-start | bytes 737280 | tf_op jit(solution)/shard_map/reduce_scatter | solution.py:252
  663.4 146.9 %reduce-scatter.16.cloned.1.call-start = ((), (), s32[]{:S(2)}) async-start(), calls=%async_computation.12 | async-start | bytes 4718592 | tf_op jit(solution)/shard_map/reduce_scatter | solution.py:164
  672.5 160.2 %reduce-scatter.30.cloned.1.call-start = ((), (), s32[]{:S(2)}) async-start(), calls=%async_computation.21 | async-start | bytes 122880
  675.7 242.0 %all-reduce.6.cloned.1.call-start = ((), (), s32[]{:S(2)}) async-start(), calls=%async_computation.22 | async-start | bytes 3833856 | tf_op jit(solution)/shard_map/psum | solution.py:266
  764.6 197.6 %reduce-scatter.20.cloned.1.call-start = ((), (), s32[]{:S(2)}) async-start(), calls=%async_computation.16 | async-start | bytes 4718592 | tf_op jit(solution)/shard_map/reduce_scatter | solution.py:222
  764.7 7.1 copy-start.64
  780.8 29.5 %copy-start.12 = (f32[2,512,767]{2,1,0:T(8,128)S(1)}, f32[2,512,767]{2,1,0:T(8,128)}, u32[]{:S(2)}) copy-start(f32[2,512,767]{2,1,0:T(8,128)} %get-tuple-element.243) | copy-start | bytes 9424900
  780.8 29.5 %copy-start.55 = (f32[767]{0:T(1024)S(1)}, f32[767]{0:T(1024)}, u32[]{:S(2)}) copy-start(f32[767]{0:T(1024)} %get-tuple-element.192) | copy-start | bytes 9208
  818.2 144.0 %copy-start.10 = (f32[2,512,767]{2,1,0:T(8,128)S(1)}, f32[2,512,767]{2,1,0:T(8,128)}, u32[]{:S(2)}) copy-start(f32[2,512,767]{2,1,0:T(8,128)} %convert_element_type.195) | copy-start | bytes 9424900
  818.2 144.0 %copy-start.41 = (f32[768]{0:T(1024)S(1)}, f32[768]{0:T(1024)}, u32[]{:S(2)}) copy-start(f32[768]{0:T(1024)} %copy-done.40) | copy-start | bytes 9220
  818.2 144.0 %copy-start.46 = (f32[2,512]{1,0:T(2,128)S(1)}, f32[2,512]{1,0:T(2,128)}, u32[]{:S(2)}) copy-start(f32[2,512]{1,0:T(2,128)} %copy-done.45) | copy-start | bytes 12292
  923.8 41.2 %copy-start.50 = (f32[1024]{0:T(1024)S(1)}, f32[1024]{0:T(1024)}, u32[]{:S(2)}) copy-start(f32[1024]{0:T(1024)} %copy-done.49) | copy-start | bytes 12292
  972.1 47.2 %copy-start.1 = (bf16[768,1536]{1,0:T(8,128)(2,1)S(1)}, bf16[768,1536]{1,0:T(8,128)(2,1)}, u32[]{:S(2)}) copy-start(bf16[768,1536]{1,0:T(8,128)(2,1)} %param.21) | copy-start | bytes 7077892
  (69 other events, 225.6 us)
Sparse Core Ops, SparseCore 0:
  28.5 47.6 all-gather.4
  184.0 43.3 reduce-scatter.13
  229.0 44.8 all-gather.8
  275.3 44.9 all-gather.6
  356.0 43.3 reduce-scatter.17
  412.4 44.8 all-gather.10
  638.6 29.3 reduce-scatter.27
  670.7 33.0 reduce-scatter.25
  706.3 33.0 reduce-scatter.23
  742.5 22.0 reduce-scatter.21
  766.9 43.3 reduce-scatter.15
  813.2 19.5 reduce-scatter.29
  836.0 81.7 all-reduce.5
  919.8 42.3 reduce-scatter.19
where the time goes:
time: 1040 us; the launch traced here: 1030 us
  waiting for transfers between devices  468 us (45%)
  matrix products  207 us (20%)
  local copies, waits for them, and re-layouts  161 us (15%)
  other arithmetic  114 us (11%)
  blocking collectives  57.5 us (6%)
  between operations  15.8 us (2%)
    psum x1, waiting for transfers between devices, on_device(): lax.psum(shards[0].astype(jnp.bfloat16), 'group').astype(jnp.float32)  71.2 us
    unnamed x134, local copies, waits for them, and re-layouts  50.8 us
    all_gather x1, waiting for transfers between devices, on_device(): full_one = lax.all_gather(one_low, 'tensor', axis=1, tiled=True)  47.5 us
    all_gather x1, waiting for transfers between devices, on_device(): lax.all_gather(branch_seq, 'tensor', axis=1, tiled=True)  44.9 us
    reduce_scatter x1, waiting for transfers between devices, on_device(): lax.psum_scatter(branch_part.astype(jnp.bfloat16), 'tensor', scatter_dime...  42.1 us
    psum x1, blocking collectives, on_device(): lax.psum((gain_terms, bias_terms), ('dp', 'group', 'tensor'))  39.6 us
    all_gather x1, waiting for transfers between devices, on_device(): lax.all_gather(two_low, 'tensor', axis=1, tiled=True)  39.4 us
    reduce_scatter x1, waiting for transfers between devices, on_device(): lax.psum_scatter(two_part.astype(jnp.bfloat16), 'tensor', scatter_dimensi...  37.4 us
  transfers between devices with their start and end apart: 14, of which 13 were waited for; matrix products, arithmetic and copies ran while one was open for 10% of the time, Pallas kernels for 0%

commit v1 on v0

--- a/solution.py
+++ b/solution.py
@@ -7,6 +7,11 @@
 HD = 64
 EPSILON = 1e-05
 MASKED = -1e30
+
+
+def add_all(block, name):
+    shards = lax.all_gather(block, name)
+    return jnp.sum(shards, axis=0)
 
 
 def decompress(compact):
@@ -263,7 +268,7 @@
         ).astype(jnp.float32),
     )
     reduced = (
-        lax.psum(shards[0].astype(jnp.bfloat16), "group").astype(jnp.float32),
+        add_all(shards[0].astype(jnp.bfloat16), "group").astype(jnp.float32),
         lax.psum(shards[1].astype(jnp.bfloat16), "group").astype(jnp.float32),
         lax.psum(shards[2].astype(jnp.bfloat16), "group").astype(jnp.float32),
         lax.psum(shards[3].astype(jnp.bfloat16), "group").astype(jnp.float32),

time: 1040 us -> 979 us (0.941)
  waiting for transfers between devices: 468 us -> 399 us
    all_gather x0 -> x1, waiting for transfers between devices: none -> 35.8 us  [add_all(): shards = lax.all_gather(block, name)]
    reduce_scatter x1, waiting for transfers between devices: 35.6 us -> 0.02 us  [on_device(): lax.psum_scatter(weight_grads[3].astype(jnp.bfloat16), 'dp', scatter_dime...]
    unnamed x16 -> x17, waiting for transfers between devices: 15.4 us -> 41 us
    reduce_scatter x1, waiting for transfers between devices: 25.3 us -> 0.02 us  [on_device(): lax.psum_scatter(weight_grads[5].astype(jnp.bfloat16), 'dp', scatter_dime...]
    reduce_scatter x1, waiting for transfers between devices: 25.2 us -> 0.02 us  [on_device(): lax.psum_scatter(weight_grads[2].astype(jnp.bfloat16), 'dp', scatter_dime...]
    all_gather x1, waiting for transfers between devices: 44.9 us -> 21.8 us  [on_device(): lax.all_gather(branch_seq, 'tensor', axis=1, tiled=True)]
    psum x1, waiting for transfers between devices: 71.2 us -> 50.2 us  [on_device(): lax.psum(shards[2].astype(jnp.bfloat16), 'group').astype(jnp.float32)]
    unnamed x134 -> x136, local copies, waits for them, and re-layouts: 50.8 us -> 54.4 us
  transfers between devices with their start and end apart: 14 -> 15, of which waited for: 13 -> 12; matrix products, arithmetic and copies ran while one was open for 10% -> 29% of each run, Pallas kernels for 0% -> 0%
where the time goes in v1:
time: 979 us; the launch traced here: 966 us
  waiting for transfers between devices  399 us (41%)
  matrix products  209 us (21%)
  local copies, waits for them, and re-layouts  164 us (17%)
  other arithmetic  117 us (12%)
  blocking collectives  58.5 us (6%)
  between operations  15.5 us (2%)
    unnamed x136, local copies, waits for them, and re-layouts  54.4 us
    psum x1, waiting for transfers between devices, on_device(): lax.psum(shards[2].astype(jnp.bfloat16), 'group').astype(jnp.float32)  50.2 us
    all_gather x1, waiting for transfers between devices, on_device(): full_one = lax.all_gather(one_low, 'tensor', axis=1, tiled=True)  47.5 us
    reduce_scatter x1, waiting for transfers between devices, on_device(): lax.psum_scatter(branch_part.astype(jnp.bfloat16), 'tensor', scatter_dime...  42.1 us
    unnamed x17, waiting for transfers between devices  41 us
    psum x1, blocking collectives, on_device(): lax.psum((gain_terms, bias_terms), ('dp', 'group', 'tensor'))  39.6 us
    all_gather x1, waiting for transfers between devices, on_device(): lax.all_gather(two_low, 'tensor', axis=1, tiled=True)  39.4 us
    reduce_scatter x1, waiting for transfers between devices, on_device(): lax.psum_scatter(one_part.astype(jnp.bfloat16), 'tensor', scatter_dimensi...  37.4 us
  transfers between devices with their start and end apart: 15, of which 12 were waited for; matrix products, arithmetic and copies ran while one was open for 29% of the time, Pallas kernels for 0%

profile of v1, /device:TPU:0, one launch (start us, length us, event | category | flops | bytes accessed | tf_op | source)
XLA Modules:
  0.0 966.5 jit_solution(8114001428074798651)
XLA Ops:
  28.7 47.5 %all-gather.7.cloned.1.call-done = bf16[2,1024,768]{2,1,0:T(8,128)(2,1)} async-done(((bf16[2,512,768]{2,1,0:T(8,128)(2,1)}), bf16[2,1024,768]{2,1,0:T(8,128)(2,1)}) %all-gather.7.cloned.1.call-update) | async-done | bytes 3145744 | tf_op jit(solution)/shard_map/all_gather | solution.py:133
  124.6 54.3 %while.26 = (s32[]{:T(128)}, bf16[2,1024,6,64]{1,3,2,0:T(8,128)(2,1)}, f32[2,6,1024]{2,1,0:T(8,128)}, bf16[2,1024,6,64]{1,3,2,0:T(8,128)(2,1)}, s32[2,1024]{1,0:...) while((s32[]{:T(128)}, ...), condition=%wide.region_7.8_spmd, body=%wide.region_2.7_spmd.sunk | while | flops 1692272128 | bytes 111457016 | solution.py:149
  185.3 42.1 %reduce-scatter.14.cloned.1.call-done = bf16[2,512,767]{2,1,0:T(8,128)(2,1)} async-done(((bf16[2,1024,767]{2,1,0:T(8,128)(2,1)}), bf16[2,512,767]{2,1,0:T(8,128)(2,1)}) %reduce-scatter.14.cloned.1.call-update) | async-done | bytes 1570832 | tf_op jit(solution)/shard_map/reduce_scatter | solution.py:154
  244.4 29.4 %all-gather.11.cloned.1.call-done = bf16[2,1024,767]{1,0,2:T(2,128)(2,1)} async-done(((bf16[2,512,767]{1,0,2:T(2,128)(2,1)}), bf16[2,1024,767]{1,0,2:T(2,128)(2,1)}) %all-gather.11.cloned.1.call-update) | async-done | bytes 3141648 | tf_op jit(solution)/shard_map/all_gather | solution.py:177
  280.9 39.4 %all-gather.9.cloned.1.call-done = bf16[2,1024,768]{2,1,0:T(8,128)(2,1)} async-done(((bf16[2,512,768]{2,1,0:T(8,128)(2,1)}), bf16[2,1024,768]{2,1,0:T(8,128)(2,1)}) %all-gather.9.cloned.1.call-update) | async-done | bytes 3145744 | tf_op jit(solution)/shard_map/all_gather | solution.py:160
  320.3 13.9 %multiply_convert_fusion.2 = (bf16[2048,1536]{1,0:T(8,128)(2,1)}, f32[2048,1536]{1,0:T(8,128)}) fusion(f32[1536]{0:T(1024)S(1)} %convert_element_type.210, bf16[2048,768]{1,0:T(8,128)(2,1)} %bitcast.355, bf16[768,1536]{1,0:T(8,128)(2,1)S(1)} %copy-done), kind=kOutput, calls=%fused_computation.125 | convolution fusion | flops 4863295488 | bytes 24385536 | tf_op jit(solution)/shard_map/dot_general | solution.py:161
  334.2 15.3 %fusion.97 = (bf16[1536]{0:T(1024)(128)(2,1)}, bf16[2048,1536]{1,0:T(8,128)(2,1)S(1)}) fusion(f32[2048,1536]{1,0:T(8,128)} %get-tuple-element.272, f32[1536]{0:T(1024)S(1)} %convert_element_type.210, bf16[2048,767]{0,1:T(8,128)(2,1)S(1)} %bitcast.322, bf16[1536,767]{1,0:T(8,128)(2,1)S(1)} %copy-done.64), kind=kOutput, calls=%fused_computation.195 | convolution fusion | flops 4894751232 | bytes 24381440 | tf_op jit(solution)/shard_map/dot_general | solution.py:182
  362.1 37.4 %reduce-scatter.18.cloned.1.call-done = bf16[2,512,768]{2,1,0:T(8,128)(2,1)} async-done(((bf16[2,1024,768]{2,1,0:T(8,128)(2,1)}), bf16[2,512,768]{2,1,0:T(8,128)(2,1)}) %reduce-scatter.18.cloned.1.call-update) | async-done | bytes 1572880 | tf_op jit(solution)/shard_map/reduce_scatter | solution.py:191
  412.5 9.2 convolution_convert_fusion
  426.3 9.2 convolution_convert_fusion.1
  435.7 21.8 %all-gather.13.cloned.1.call-done = bf16[2,1024,767]{1,0,2:T(2,128)(2,1)} async-done(((bf16[2,512,767]{1,0,2:T(2,128)(2,1)}), bf16[2,1024,767]{1,0,2:T(2,128)(2,1)}) %all-gather.13.cloned.1.call-update) | async-done | bytes 3141648 | tf_op jit(solution)/shard_map/all_gather | solution.py:199
  472.7 134.3 %while.27 = (s32[]{:T(128)}, bf16[2,1024,6,64]{1,3,2,0:T(8,128)(2,1)}, bf16[2,1024,6,64]{1,3,2,0:T(8,128)(2,1)}, bf16[2,1024,6,64]{1,3,2,0:T(8,128)(2,1)}, bf16[...) while((s32[]{:T(128)}, ...), condition=%wide.region_17.18_spmd, body=%wide.region_14.17_spmd.sunk | while | flops 4128632320 | bytes 286275584 | solution.py:208
  492.7 8.5 multiply_reduce_fusion.10
  501.1 9.7 %multiply_convert_fusion.7 = bf16[6,512,1024]{2,1,0:T(8,128)(2,1)} fusion(f32[6,512,1024]{2,1,0:T(8,128)} %get-tuple-element.417, f32[6,512,1024]{2,1,0:T(8,128)S(1)} %fusion.175, f32[6,512]{1,0:T(8,128)S(1)} %get-tuple-element.418, f32[6,512]{1,0:T(8,128)S(1)} %get-tuple-element.411, pred[512,1024]{1,0:T(8,128)(4,1)S(1)} %get-tuple-element.416), kind=kLoop, calls=%fused_computation.51.clone.1 | loop fusion | flops 18874368 | bytes 32006144 | tf_op jit(solution)/shard_map/while/body/eval_jaxpr/convert_element_type | solution.py:85
  516.4 8.1 multiply_reduce_fusion.11
  524.5 7.1 multiply_convert_fusion.8
  559.8 8.4 multiply_reduce_fusion.10
  568.3 9.7 %multiply_convert_fusion.7 = bf16[6,512,1024]{2,1,0:T(8,128)(2,1)} fusion(f32[6,512,1024]{2,1,0:T(8,128)} %get-tuple-element.417, f32[6,512,1024]{2,1,0:T(8,128)S(1)} %fusion.175, f32[6,512]{1,0:T(8,128)S(1)} %get-tuple-element.418, f32[6,512]{1,0:T(8,128)S(1)} %get-tuple-element.411, pred[512,1024]{1,0:T(8,128)(4,1)S(1)} %get-tuple-element.416), kind=kLoop, calls=%fused_computation.51.clone.1 | loop fusion | flops 18874368 | bytes 32006144 | tf_op jit(solution)/shard_map/while/body/eval_jaxpr/convert_element_type | solution.py:85
  583.2 8.1 multiply_reduce_fusion.11
  591.3 7.0 multiply_convert_fusion.8
  632.9 7.4 convert_bitcast_fusion.1
  645.8 9.2 convolution_convert_fusion.3
  659.0 25.0 %reduce-scatter.28.cloned.1.call-done = bf16[192,1152]{1,0:T(8,128)(2,1)} async-done(((bf16[768,1152]{1,0:T(8,128)(2,1)}), bf16[192,1152]{1,0:T(8,128)(2,1)}) %reduce-scatter.28.cloned.1.call-update) | async-done | bytes 442384
  693.1 8.2 bitcast_convert_fusion
  706.3 6.8 all-reduce
  713.2 16.5 %reduce-scatter.16.cloned.1.call-done = bf16[2,512,767]{2,1,0:T(8,128)(2,1)} async-done(((bf16[2,1024,767]{2,1,0:T(8,128)(2,1)}), bf16[2,512,767]{2,1,0:T(8,128)(2,1)}) %reduce-scatter.16.cloned.1.call-update) | async-done | bytes 1570832 | tf_op jit(solution)/shard_map/reduce_scatter | solution.py:169
  737.7 14.5 %reduce-scatter.30.cloned.1.call-done = bf16[96,2]{1,0:T(8,128)(2,1)} async-done(((bf16[384,2]{1,0:T(8,128)(2,1)}), bf16[96,2]{1,0:T(8,128)(2,1)}) %reduce-scatter.30.cloned.1.call-update) | async-done | bytes 400
  752.9 12.1 %all-reduce.2 = (bf16[2,96]{1,0:T(2,128)(2,1)S(1)}, bf16[384]{0:T(512)(128)(2,1)S(1)}) all-reduce(bf16[2,96]{1,0:T(2,128)(2,1)S(1)} %copy.97, bf16[384]{0:T(512)(128)(2,1)S(1)} %dynamic-slice.1), channel_id=1, replica_groups=mesh['dp'=4,'group'=4,'tensor'=2] {'group'}, use_global_device_ids=true, to_apply=%region_28.29 | all-reduce | flops 576 | bytes 2304 | tf_op jit(solution)/shard_map/psum | solution.py:272
  766.2 50.2 %all-reduce.6.cloned.1.call-done = (bf16[96,767]{1,0:T(8,128)(2,1)}, bf16[192,1536]{1,0:T(8,128)(2,1)}, bf16[384,767]{1,0:T(8,128)(2,1)}) async-done(((bf16[96,767]{1,0:T(8,128)(2,1)}, bf16[192,1536]{1,0:T(8,128)(2,1)}, bf16[384,767]{1,0:T(8,128)(2,1)}), (bf16[96,767]{1,0:T(8,128)(2,1)}, bf16[192,1536]{1,0:T(8,128)(2,1)}, bf16[384,767]{1,0:T(8,128)(2,1)})) %all-reduce.6.cloned.1.call-update) | async-done | bytes 1326160 | tf_op jit(solution)/shard_map/psum | solution.py:273
  822.5 35.8 %all-gather.15.cloned.1.call-done = bf16[12,192,384]{2,1,0:T(8,128)(2,1)} async-done(((bf16[3,192,384]{2,1,0:T(8,128)(2,1)}), bf16[12,192,384]{2,1,0:T(8,128)(2,1)}) %all-gather.15.cloned.1.call-update) | async-done | bytes 1769488 | tf_op jit(solution)/shard_map/all_gather | solution.py:13
  865.2 37.4 %reduce-scatter.20.cloned.1.call-done = bf16[2,512,768]{2,1,0:T(8,128)(2,1)} async-done(((bf16[2,1024,768]{2,1,0:T(8,128)(2,1)}), bf16[2,512,768]{2,1,0:T(8,128)(2,1)}) %reduce-scatter.20.cloned.1.call-update) | async-done | bytes 1572880 | tf_op jit(solution)/shard_map/reduce_scatter | solution.py:227
  920.1 39.6 %all-reduce.1 = (f32[2,768]{1,0:T(2,128)}, f32[2,767]{1,0:T(2,128)}) all-reduce(f32[2,768]{1,0:T(2,128)S(1)} %pad_maximum_fusion.4, f32[2,767]{1,0:T(2,128)S(1)} %pad_maximum_fusion.5), channel_id=1, replica_groups=mesh['dp'=4,'group'=4,'tensor'=2] {'dp','group','tensor'}, use_global_device_ids=true, to_apply=%region_22.23 | all-reduce | flops 3070 | bytes 24560 | tf_op jit(solution)/shard_map/psum | solution.py:241
  (394 shorter events, 355.1 us)
Async XLA Ops:
  7.2 313.1 %copy-start = (bf16[768,1536]{1,0:T(8,128)(2,1)S(1)}, bf16[768,1536]{1,0:T(8,128)(2,1)}, u32[]{:S(2)}) copy-start(bf16[768,1536]{1,0:T(8,128)(2,1)} %param.21) | copy-start | bytes 7077892
  7.2 69.0 %all-gather.7.cloned.1.call-start = ((), (), s32[]{:S(2)}) async-start(), calls=%async_computation.9 | async-start | bytes 4718592 | tf_op jit(solution)/shard_map/all_gather | solution.py:133
  28.5 198.9 %reduce-scatter.14.cloned.1.call-start = ((), (), s32[]{:S(2)}) async-start(), calls=%async_computation.10 | async-start | bytes 4718592 | tf_op jit(solution)/shard_map/reduce_scatter | solution.py:154
  124.6 54.4 %copy-start.66 = (bf16[384,767]{1,0:T(8,128)(2,1)S(1)}, bf16[384,767]{1,0:T(8,128)(2,1)}, u32[]{:S(2)}) copy-start(bf16[384,767]{1,0:T(8,128)(2,1)} %param.20) | copy-start | bytes 1767172
  183.8 90.0 %all-gather.11.cloned.1.call-start = ((), (), s32[]{:S(2)}) async-start(), calls=%async_computation.13 | async-start | bytes 4712448 | tf_op jit(solution)/shard_map/all_gather | solution.py:177
  184.6 135.7 %all-gather.9.cloned.1.call-start = ((), (), s32[]{:S(2)}) async-start(), calls=%async_computation.11 | async-start | bytes 4718592 | tf_op jit(solution)/shard_map/all_gather | solution.py:160
  231.7 9.2 copy-start.31
  244.4 155.1 %reduce-scatter.18.cloned.1.call-start = ((), (), s32[]{:S(2)}) async-start(), calls=%async_computation.14 | async-start | bytes 4718592 | tf_op jit(solution)/shard_map/reduce_scatter | solution.py:191
  320.3 13.9 %copy-start.34 = (bf16[96,8,2,1024]{3,1,2,0:T(8,128)(2,1)S(1)}, bf16[96,8,2,1024]{3,1,2,0:T(8,128)(2,1)}, u32[]{:S(2)}) copy-start(bf16[96,8,2,1024]{3,1,2,0:T(8,128)(2,1)} %copy.103) | copy-start | bytes 9437188
  320.3 13.9 %copy-start.64 = (bf16[1536,767]{1,0:T(8,128)(2,1)S(1)}, bf16[1536,767]{1,0:T(8,128)(2,1)}, u32[]{:S(2)}) copy-start(bf16[1536,767]{1,0:T(8,128)(2,1)} %param.23) | copy-start | bytes 7068676
  356.0 101.4 %all-gather.13.cloned.1.call-start = ((), (), s32[]{:S(2)}) async-start(), calls=%async_computation.15 | async-start | bytes 4712448 | tf_op jit(solution)/shard_map/all_gather | solution.py:199
  359.6 39.9 %copy-start.11 = (f32[2,512,767]{2,1,0:T(8,128)S(1)}, f32[2,512,767]{2,1,0:T(8,128)}, u32[]{:S(2)}) copy-start(f32[2,512,767]{2,1,0:T(8,128)} %get-tuple-element.242) | copy-start | bytes 9424900
  412.4 245.8 %reduce-scatter.26.cloned.1.call-start = ((), (), s32[]{:S(2)}) async-start(), calls=%async_computation.19 | async-start | bytes 2949120 | tf_op jit(solution)/shard_map/reduce_scatter | solution.py:266
  421.7 236.5 %reduce-scatter.24.cloned.1.call-start = ((), (), s32[]{:S(2)}) async-start(), calls=%async_computation.18 | async-start | bytes 2949120 | tf_op jit(solution)/shard_map/reduce_scatter | solution.py:260
  435.6 222.7 %reduce-scatter.22.cloned.1.call-start = ((), (), s32[]{:S(2)}) async-start(), calls=%async_computation.17 | async-start | bytes 737280 | tf_op jit(solution)/shard_map/reduce_scatter | solution.py:257
  476.5 10.7 %copy-start.5 = (pred[512,1024]{1,0:T(8,128)(4,1)}, pred[512,1024]{1,0:T(8,128)(4,1)S(1)}, u32[]{:S(2)}) copy-start(pred[512,1024]{1,0:T(8,128)(4,1)S(1)} %get-tuple-element.420) | copy-start | bytes 1572868 | tf_op jit(solution)/shard_map/while
  524.5 7.1 copy-start.4
  543.7 10.6 %copy-start.5 = (pred[512,1024]{1,0:T(8,128)(4,1)}, pred[512,1024]{1,0:T(8,128)(4,1)S(1)}, u32[]{:S(2)}) copy-start(pred[512,1024]{1,0:T(8,128)(4,1)S(1)} %get-tuple-element.420) | copy-start | bytes 1572868 | tf_op jit(solution)/shard_map/while
  591.3 7.0 copy-start.4
  629.6 54.3 %reduce-scatter.28.cloned.1.call-start = ((), (), s32[]{:S(2)}) async-start(), calls=%async_computation.21 | async-start | bytes 2211840
  645.7 84.0 %reduce-scatter.16.cloned.1.call-start = ((), (), s32[]{:S(2)}) async-start(), calls=%async_computation.12 | async-start | bytes 4718592 | tf_op jit(solution)/shard_map/reduce_scatter | solution.py:169
  655.0 97.1 %reduce-scatter.30.cloned.1.call-start = ((), (), s32[]{:S(2)}) async-start(), calls=%async_computation.22 | async-start | bytes 122880
  658.2 158.2 %all-reduce.6.cloned.1.call-start = ((), (), s32[]{:S(2)}) async-start(), calls=%async_computation.23 | async-start | bytes 2654208 | tf_op jit(solution)/shard_map/psum | solution.py:273
  658.9 199.4 %all-gather.15.cloned.1.call-start = ((), (), s32[]{:S(2)}) async-start(), calls=%async_computation.20 | async-start | bytes 2211840 | tf_op jit(solution)/shard_map/all_gather | solution.py:13
  686.3 216.4 %reduce-scatter.20.cloned.1.call-start = ((), (), s32[]{:S(2)}) async-start(), calls=%async_computation.16 | async-start | bytes 4718592 | tf_op jit(solution)/shard_map/reduce_scatter | solution.py:227
  701.3 28.3 %copy-start.12 = (f32[2,512,767]{2,1,0:T(8,128)S(1)}, f32[2,512,767]{2,1,0:T(8,128)}, u32[]{:S(2)}) copy-start(f32[2,512,767]{2,1,0:T(8,128)} %get-tuple-element.242) | copy-start | bytes 9424900
  701.4 28.4 %copy-start.56 = (f32[767]{0:T(1024)S(1)}, f32[767]{0:T(1024)}, u32[]{:S(2)}) copy-start(f32[767]{0:T(1024)} %get-tuple-element.192) | copy-start | bytes 9208
  820.2 82.5 %copy-start.10 = (f32[2,512,767]{2,1,0:T(8,128)S(1)}, f32[2,512,767]{2,1,0:T(8,128)}, u32[]{:S(2)}) copy-start(f32[2,512,767]{2,1,0:T(8,128)} %convert_element_type.197) | copy-start | bytes 9424900
  820.2 82.5 %copy-start.42 = (f32[768]{0:T(1024)S(1)}, f32[768]{0:T(1024)}, u32[]{:S(2)}) copy-start(f32[768]{0:T(1024)} %copy-done.41) | copy-start | bytes 9220
  820.2 82.5 %copy-start.47 = (f32[2,512]{1,0:T(2,128)S(1)}, f32[2,512]{1,0:T(2,128)}, u32[]{:S(2)}) copy-start(f32[2,512]{1,0:T(2,128)} %copy-done.46) | copy-start | bytes 12292
  863.0 42.4 %copy-start.51 = (f32[1024]{0:T(1024)S(1)}, f32[1024]{0:T(1024)}, u32[]{:S(2)}) copy-start(f32[1024]{0:T(1024)} %copy-done.50) | copy-start | bytes 12292
  912.5 47.2 %copy-start.1 = (bf16[768,1536]{1,0:T(8,128)(2,1)S(1)}, bf16[768,1536]{1,0:T(8,128)(2,1)}, u32[]{:S(2)}) copy-start(bf16[768,1536]{1,0:T(8,128)(2,1)} %param.21) | copy-start | bytes 7077892
  (71 other events, 231.3 us)
Sparse Core Ops, SparseCore 0:
  28.6 47.6 all-gather.6
  184.0 43.3 reduce-scatter.13
  229.0 44.8 all-gather.10
  275.3 44.9 all-gather.8
  356.1 43.3 reduce-scatter.17
  412.5 44.8 all-gather.12
  460.0 33.0 reduce-scatter.25
  495.8 33.0 reduce-scatter.23
  629.8 22.3 reduce-scatter.21
  654.5 29.3 reduce-scatter.27
  686.3 43.3 reduce-scatter.15
  732.5 19.5 reduce-scatter.29
  754.7 61.5 all-reduce.5
  818.3 39.9 all-gather.14
  860.4 42.2 reduce-scatter.19
